TPU v7x, 32 devices: a whole 2x2x4 slice. The times are simulated.
32 devices in a mesh: dp: 8 (over z, x), fsdp: 4 (over y, core).
Axes of the slice: x: 2, y: 2, z: 4, core: 2. Of those that a mesh axis runs over, the one named last changes fastest.
Arguments:
- hidden_in: float32 [32, 496, 768], P(('dp', 'fsdp')), may hold values from -6 to 6
- cotangent: float32 [32, 496, 768], P(('dp', 'fsdp')), may hold values from -6 to 6
- lengths: int32 [32], P(('dp', 'fsdp')), may hold values from 397 to 496, as said below
- qkv_weight: float32 [2, 768, 2304], P(None, ('dp', 'fsdp')), may hold values from -0.21875 to 0.21875
- out_weight: float32 [2, 768, 768], P(None, ('dp', 'fsdp')), may hold values from -6 to 6
- up_weight: float32 [2, 768, 3072], P(None, ('dp', 'fsdp')), may hold values from -0.21875 to 0.21875
- down_weight: float32 [2, 3072, 768], P(None, None, ('dp', 'fsdp')), may hold values from -0.109375 to 0.109375
- norm_gains: float32 [2, 2, 768], P(None, None, ('dp', 'fsdp')), may hold values from 0.5 to 1.5
- biases: float32 [2, 6, 768], P(None, None, ('dp', 'fsdp')), may hold values from -1.2 to 1.2
- up_bias: float32 [2, 3072], P(None, ('dp', 'fsdp')), may hold values from -1.2 to 1.2
Outputs:
- output: float32 [32, 496, 768], P(('dp', 'fsdp'))
- input_grad: float32 [32, 496, 768], P(('dp', 'fsdp'))
- qkv_grad: float32 [2, 768, 2304], P(None, ('dp', 'fsdp'))
- out_grad: float32 [2, 768, 768], P(None, ('dp', 'fsdp'))
- up_grad: float32 [2, 768, 3072], P(None, ('dp', 'fsdp'))
- down_grad: float32 [2, 3072, 768], P(None, None, ('dp', 'fsdp'))
- gains_grad: float32 [2, 2, 768], P(None, None, ('dp', 'fsdp'))
- biases_grad: float32 [2, 6, 768], P(None, None, ('dp', 'fsdp'))
- up_bias_grad: float32 [2, 3072], P(None, ('dp', 'fsdp'))
Inputs may be any that keep to these rules, and one draw needn't show every extreme that they name: `lengths`: valid patches of each clip; some clip has exactly 496.
All inputs are finite; a program needn't handle non-finite values.
Results may differ from a plain program's by a relative error of at most 0.013.
Values may be sent and summed in bfloat16 or wider, within the bound.
No kernel may reach another device: no remote copies, remote signals or barrier semaphores. Data moves between devices by JAX's collectives and lax.ppermute only.
A program may use at most 320 MiB of HBM per device.

v0:
```python
import jax
import jax.numpy as jnp
from jax import lax
from jax.sharding import PartitionSpec as P

HEADS = 12
HEAD_WIDTH = 64
norm_eps = 1e-06
section_kinds = ("rows", "rows", "rows", "cols", "cols", "flat", "cols")


def layer_norm(values, gain, shift):
    center = values - jnp.mean(values, axis=-1, keepdims=True)
    spread = jnp.mean(center * center, axis=-1, keepdims=True)
    return center * lax.rsqrt(spread + norm_eps) * gain + shift


def gelu_exact(values):
    return jax.nn.gelu(values, approximate=False)


def pack_owned(pieces):
    return jnp.concatenate([piece.reshape(1, -1) for piece in pieces], axis=1)


def unpack_whole(gathered, shapes):
    count = gathered.shape[0]
    result = []
    offset = 0
    for shape, kind in zip(shapes, section_kinds):
        length = 1
        for extent in shape:
            length = length * extent
        section = gathered[:, offset : offset + length]
        offset = offset + length
        if kind == "rows":
            result.append(section.reshape((count * shape[0],) + tuple(shape[1:])))
        elif kind == "cols":
            result.append(
                section.reshape(count, shape[0], shape[1])
                .transpose(1, 0, 2)
                .reshape(shape[0], count * shape[1])
            )
        else:
            result.append(section.reshape(count * shape[0]))
    return tuple(result)


def pack_blocks(grads, count):
    pieces = []
    for grad, kind in zip(grads, section_kinds):
        if kind == "cols":
            pieces.append(
                grad.reshape(grad.shape[0], count, -1).transpose(1, 0, 2).reshape(count, -1)
            )
        else:
            pieces.append(grad.reshape(count, -1))
    return jnp.concatenate(pieces, axis=1)


def unpack_owned(owned_row, shapes):
    result = []
    offset = 0
    for shape in shapes:
        length = 1
        for extent in shape:
            length = length * extent
        result.append(owned_row[0, offset : offset + length].reshape(shape))
        offset = offset + length
    return tuple(result)


def collect(w_qkv, w_out, w_up, w_down, gains, up_shift, shifts):
    pieces = (w_qkv, w_out, w_up, w_down, gains, up_shift, shifts)
    shapes = [piece.shape for piece in pieces]
    owned_row = pack_owned(pieces)
    gathered = lax.all_gather(owned_row, ("dp", "fsdp"), axis=0, tiled=True)
    return unpack_whole(gathered, shapes)


def spread_grads(grads, shapes):
    count = lax.axis_size("dp") * lax.axis_size("fsdp")
    blocks = pack_blocks(grads, count)
    owned_row = lax.psum_scatter(blocks, ("dp", "fsdp"), scatter_dimension=0, tiled=True)
    return unpack_owned(owned_row, shapes)


def split_heads(qkv_rows, clips, slots):
    parts = qkv_rows.reshape(clips, slots, 3, HEADS, HEAD_WIDTH)
    return (parts[:, :, 0], parts[:, :, 1], parts[:, :, 2])


def masked_scores(query_matrix, key_matrix, valid):
    attention_scores = jnp.einsum(
        "clhd,cmhd->chlm", query_matrix, key_matrix, preferred_element_type=jnp.float32
    ) * HEAD_WIDTH ** (-0.5)
    return jnp.where(valid[:, None, None, :], attention_scores, -1e30)


def forward_layer(residual, matrices, valid, clips, slots):
    w_qkv, w_out, w_up, w_down, gains_low, up_low, shifts_low = matrices
    gains = gains_low.astype(jnp.float32)
    shifts = shifts_low.astype(jnp.float32)
    normed = layer_norm(residual, gains[0], shifts[4]).astype(jnp.bfloat16)
    qkv_bias = jnp.concatenate([shifts[0], jnp.zeros_like(shifts[0]), shifts[1]])
    qkv_rows = (jnp.dot(normed, w_qkv, preferred_element_type=jnp.float32) + qkv_bias).astype(
        jnp.bfloat16
    )
    query_matrix, key_matrix, value_matrix = split_heads(qkv_rows, clips, slots)
    masked = masked_scores(query_matrix, key_matrix, valid)
    peak = jnp.max(masked, axis=-1, keepdims=True)
    expo = jnp.exp(masked - peak)
    total = jnp.sum(expo, axis=-1, keepdims=True)
    attention_probabilities = (expo / total).astype(jnp.bfloat16)
    log_total = peak + jnp.log(total)
    mixed = jnp.einsum(
        "chlm,cmhd->clhd", attention_probabilities, value_matrix, preferred_element_type=jnp.float32
    )
    mixed = mixed.reshape(clips * slots, residual.shape[1]).astype(jnp.bfloat16)
    middle = residual + (jnp.dot(mixed, w_out, preferred_element_type=jnp.float32) + shifts[2])
    normed_two = layer_norm(middle, gains[1], shifts[5]).astype(jnp.bfloat16)
    hidden_pre = jnp.dot(normed_two, w_up, preferred_element_type=jnp.float32) + up_low.astype(
        jnp.float32
    )
    hidden = gelu_exact(hidden_pre).astype(jnp.bfloat16)
    result = middle + (jnp.dot(hidden, w_down, preferred_element_type=jnp.float32) + shifts[3])
    return (
        result,
        (residual, normed, qkv_rows, log_total, mixed, middle, normed_two, hidden_pre, hidden),
    )


def backward_layer(grad_result, matrices, record, valid, clips, slots):
    w_qkv, w_out, w_up, w_down, gains_low, up_low, shifts_low = matrices
    gains = gains_low.astype(jnp.float32)
    shifts = shifts_low.astype(jnp.float32)
    residual, normed, qkv_rows, log_total, mixed, middle, normed_two, hidden_pre, hidden = record
    width = residual.shape[1]
    down_low = grad_result.astype(jnp.bfloat16)
    grad_down = jnp.einsum("tf,td->fd", hidden, down_low, preferred_element_type=jnp.float32)
    grad_down_bias = jnp.sum(down_low, axis=0, dtype=jnp.float32)
    grad_hidden = jnp.einsum("td,fd->tf", down_low, w_down, preferred_element_type=jnp.float32)
    unused, gelu_pull = jax.vjp(gelu_exact, hidden_pre)
    grad_pre = gelu_pull(grad_hidden)[0].astype(jnp.bfloat16)
    grad_up = jnp.einsum("td,tf->df", normed_two, grad_pre, preferred_element_type=jnp.float32)
    grad_up_bias = jnp.sum(grad_pre, axis=0, dtype=jnp.float32)
    grad_normed_two = jnp.einsum("tf,df->td", grad_pre, w_up, preferred_element_type=jnp.float32)
    unused_two, norm_pull_two = jax.vjp(layer_norm, middle, gains[1], shifts[5])
    grad_mid_part, grad_gain_two, grad_shift_two = norm_pull_two(grad_normed_two)
    grad_middle = grad_result + grad_mid_part
    branch_low = grad_middle.astype(jnp.bfloat16)
    grad_out_weight = jnp.einsum("te,td->ed", mixed, branch_low, preferred_element_type=jnp.float32)
    grad_out_bias = jnp.sum(branch_low, axis=0, dtype=jnp.float32)
    grad_mixed = jnp.einsum(
        "td,ed->te", branch_low, w_out, preferred_element_type=jnp.float32
    ).astype(jnp.bfloat16)
    query_matrix, key_matrix, value_matrix = split_heads(qkv_rows, clips, slots)
    masked = masked_scores(query_matrix, key_matrix, valid)
    attention_probabilities = jnp.exp(masked - log_total)
    grad_heads = grad_mixed.reshape(clips, slots, HEADS, HEAD_WIDTH)
    grad_probs = jnp.einsum(
        "clhd,cmhd->chlm", grad_heads, value_matrix, preferred_element_type=jnp.float32
    )
    grad_values = jnp.einsum(
        "chlm,clhd->cmhd",
        attention_probabilities.astype(jnp.bfloat16),
        grad_heads,
        preferred_element_type=jnp.float32,
    )
    row_terms = jnp.sum(attention_probabilities * grad_probs, axis=-1, keepdims=True)
    grad_scores = (attention_probabilities * (grad_probs - row_terms)).astype(jnp.bfloat16)
    grad_queries = jnp.einsum(
        "chlm,cmhd->clhd", grad_scores, key_matrix, preferred_element_type=jnp.float32
    ) * HEAD_WIDTH ** (-0.5)
    grad_keys = jnp.einsum(
        "chlm,clhd->cmhd", grad_scores, query_matrix, preferred_element_type=jnp.float32
    ) * HEAD_WIDTH ** (-0.5)
    grad_qkv_rows = (
        jnp.stack([grad_queries, grad_keys, grad_values], axis=2)
        .reshape(clips * slots, 3 * width)
        .astype(jnp.bfloat16)
    )
    grad_qkv = jnp.einsum("td,te->de", normed, grad_qkv_rows, preferred_element_type=jnp.float32)
    grad_query_bias = jnp.sum(grad_qkv_rows[:, :width], axis=0, dtype=jnp.float32)
    grad_value_bias = jnp.sum(grad_qkv_rows[:, 2 * width :], axis=0, dtype=jnp.float32)
    grad_normed = jnp.einsum("te,de->td", grad_qkv_rows, w_qkv, preferred_element_type=jnp.float32)
    unused_one, norm_pull_one = jax.vjp(layer_norm, residual, gains[0], shifts[4])
    grad_res_part, grad_gain_one, grad_shift_one = norm_pull_one(grad_normed)
    grad_input = grad_middle + grad_res_part
    grad_gains = jnp.stack([grad_gain_one, grad_gain_two])
    grad_shifts = jnp.stack(
        [
            grad_query_bias,
            grad_value_bias,
            grad_out_bias,
            grad_down_bias,
            grad_shift_one,
            grad_shift_two,
        ]
    )
    return (
        grad_input,
        (grad_qkv, grad_out_weight, grad_up, grad_down, grad_gains, grad_up_bias, grad_shifts),
    )


def local(
    hidden_in,
    cotangent,
    lengths,
    qkv_weight,
    out_weight,
    up_weight,
    down_weight,
    norm_gains,
    biases,
    up_bias,
):
    clips, slots, width = hidden_in.shape
    layers = qkv_weight.shape[0]
    valid = lax.broadcasted_iota(jnp.int32, (clips, slots), 1) < lengths[:, None]
    owned_shapes = [
        qkv_weight.shape[1:],
        out_weight.shape[1:],
        up_weight.shape[1:],
        down_weight.shape[1:],
        norm_gains.shape[1:],
        up_bias.shape[1:],
        biases.shape[1:],
    ]

    def fetch(layer_index):
        return collect(
            qkv_weight[layer_index].astype(jnp.bfloat16),
            out_weight[layer_index].astype(jnp.bfloat16),
            up_weight[layer_index].astype(jnp.bfloat16),
            down_weight[layer_index].astype(jnp.bfloat16),
            norm_gains[layer_index].astype(jnp.bfloat16),
            up_bias[layer_index].astype(jnp.bfloat16),
            biases[layer_index].astype(jnp.bfloat16),
        )

    residual = hidden_in.reshape(clips * slots, width)
    kept_matrices = []
    records = []
    for layer_index in range(layers):
        matrices = fetch(layer_index)
        residual, record = forward_layer(residual, matrices, valid, clips, slots)
        kept_matrices.append(matrices)
        records.append(record)
    result = residual.reshape(clips, slots, width)
    grad_rows = cotangent.reshape(clips * slots, width)
    owned_grads = [None] * layers
    for layer_index in reversed(range(layers)):
        matrices = fetch(layer_index)
        grad_rows, terms = backward_layer(
            grad_rows, matrices, records[layer_index], valid, clips, slots
        )
        owned_grads[layer_index] = spread_grads(terms, owned_shapes)

    def stacked(member):
        return jnp.stack([owned_grads[layer_index][member] for layer_index in range(layers)])

    return (
        result,
        grad_rows.reshape(clips, slots, width),
        stacked(0),
        stacked(1),
        stacked(2),
        stacked(3),
        stacked(4),
        stacked(6),
        stacked(5),
    )


def solution(mesh):
    return jax.shard_map(
        local,
        mesh=mesh,
        in_specs=(
            P(("dp", "fsdp"), None, None),
            P(("dp", "fsdp"), None, None),
            P(("dp", "fsdp")),
            P(None, ("dp", "fsdp"), None),
            P(None, ("dp", "fsdp"), None),
            P(None, ("dp", "fsdp"), None),
            P(None, None, ("dp", "fsdp")),
            P(None, None, ("dp", "fsdp")),
            P(None, None, ("dp", "fsdp")),
            P(None, ("dp", "fsdp")),
        ),
        out_specs=(
            P(("dp", "fsdp"), None, None),
            P(("dp", "fsdp"), None, None),
            P(None, ("dp", "fsdp"), None),
            P(None, ("dp", "fsdp"), None),
            P(None, ("dp", "fsdp"), None),
            P(None, None, ("dp", "fsdp")),
            P(None, None, ("dp", "fsdp")),
            P(None, None, ("dp", "fsdp")),
            P(None, ("dp", "fsdp")),
        ),
        check_vma=False,
    )
```

profile of v0, /device:TPU:0, one launch (start us, length us, event | category | flops | bytes accessed | tf_op | source)
XLA Modules:
  0.0 1921.5 jit_solution(10509792829952141196)
XLA Ops:
  45.8 148.9 %all-gather.5.cloned.1.call-done = bf16[32,1,221472]{2,1,0:T(2,128)(2,1)} async-done(((bf16[1,1,221472]{2,1,0:T(2,128)(2,1)}), bf16[32,1,221472]{2,1,0:T(2,128)(2,1)}) %all-gather.5.cloned.1.call-update) | async-done | bytes 14174224 | tf_op jit(solution)/shard_map/all_gather | solution.py:77
  194.7 15.4 copy.165
  216.2 8.1 fusion.78
  224.2 142.1 %all-gather.7.cloned.1.call-done = bf16[32,1,221472]{2,1,0:T(2,128)(2,1)} async-done(((bf16[1,1,221472]{2,1,0:T(2,128)(2,1)}), bf16[32,1,221472]{2,1,0:T(2,128)(2,1)}) %all-gather.7.cloned.1.call-update) | async-done | bytes 14174224 | tf_op jit(solution)/shard_map/all_gather | solution.py:77
  366.3 15.0 copy.164
  387.9 8.0 fusion.77
  446.6 55.6 %reshape.869 = bf16[32,3072,24]{2,1,0:T(8,128)(2,1)} reshape(bf16[32,73728]{1,0:T(8,128)(2,1)} %get-tuple-element.73) | data formatting | bytes 9437184 | tf_op jit(solution)/shard_map/reshape | solution.py:40
  502.1 20.0 %copy.105 = bf16[3072,32,24]{0,2,1:T(8,128)(2,1)} copy(bf16[3072,32,24]{2,0,1:T(8,128)(2,1)} %bitcast.250) | data formatting | bytes 9437184 | tf_op jit(solution)/shard_map/transpose | solution.py:41
  527.8 20.6 %multiply_convert_fusion.3 = (bf16[496,3072]{1,0:T(8,128)(2,1)S(1)}, f32[496,3072]{1,0:T(8,128)}, f32[496,3072]{1,0:T(8,128)}) fusion(f32[3072]{0:T(1024)} %reshape.900, bf16[768,3072]{1,0:T(8,128)(2,1)} %reshape.868, f32[496,768]{1,0:T(8,128)} %copy-done.27, f32[768]{0:T(1024)} %add.213, f32[768]{0:T(1024)} %mul.380, f32[496]{0:T(512)} %fusion.53, ...), kind=kOutput, calls=%fused_computation.51 | convolution fusion | flops 2442891264 | bytes 21501824 | tf_op jit(solution)/shard_map/dot_general | solution.py:122
  582.1 55.6 %reshape.878 = bf16[32,3072,24]{2,1,0:T(8,128)(2,1)} reshape(bf16[32,73728]{1,0:T(8,128)(2,1)} %get-tuple-element.71) | data formatting | bytes 9437184 | tf_op jit(solution)/shard_map/reshape | solution.py:40
  637.7 19.9 %copy.119 = bf16[3072,32,24]{0,2,1:T(8,128)(2,1)} copy(bf16[3072,32,24]{2,0,1:T(8,128)(2,1)} %bitcast.251) | data formatting | bytes 9437184 | tf_op jit(solution)/shard_map/transpose | solution.py:41
  657.5 18.4 multiply_convert_fusion.2
  692.1 7.5 fusion.34
  721.3 8.0 convert_reduce_fusion.1
  736.7 7.5 fusion.37
  812.8 8.1 reshape.895
  827.8 25.7 %copy.136 = f32[32,3072,24]{2,1,0:T(8,128)} copy(f32[32,3072,24]{1,0,2:T(8,128)} %convolution_bitcast_fusion) | data formatting | bytes 18874368 | tf_op jit(solution)/shard_map/transpose | solution.py:54
  853.6 70.8 %reshape.896 = f32[32,73728]{1,0:T(8,128)} reshape(f32[32,3072,24]{2,1,0:T(8,128)} %copy.136) | data formatting | bytes 18874368 | tf_op jit(solution)/shard_map/reshape | solution.py:54
  941.3 8.1 reshape.887
  949.4 25.7 %copy.129 = f32[3072,32,24]{2,0,1:T(8,128)} copy(f32[3072,32,24]{0,2,1:T(8,128)} %bitcast.278) | data formatting | bytes 18874368 | tf_op jit(solution)/shard_map/reshape | solution.py:54
  975.1 71.1 %reshape.889 = f32[32,73728]{1,0:T(8,128)} reshape(f32[32,3072,24]{2,1,0:T(8,128)} %bitcast.249) | data formatting | bytes 18874368 | tf_op jit(solution)/shard_map/reshape | solution.py:54
  1049.0 8.5 constant_dynamic-update-slice_fusion.25
  1067.6 8.4 constant_dynamic-update-slice_fusion.15
  1095.9 795.2 %all-reduce.5.cloned.1.call-done = (f32[32,221472]{1,0:T(8,128)}, f32[32,221472]{1,0:T(8,128)}) async-done(((f32[32,221472]{1,0:T(8,128)}, f32[32,221472]{1,0:T(8,128)}), (f32[32,221472]{1,0:T(8,128)}, f32[32,221472]{1,0:T(8,128)})) %all-reduce.5.cloned.1.call-update) | async-done | bytes 56696848
  (553 shorter events, 332.8 us)
Async XLA Ops:
  7.2 187.5 %all-gather.5.cloned.1.call-start = ((), (), s32[]{:S(2)}) async-start(), calls=%async_computation | async-start | bytes 29246976 | tf_op jit(solution)/shard_map/all_gather | solution.py:77
  13.9 26.1 %copy-start.22 = (f32[1,496,768]{2,1,0:T(8,128)S(1)}, f32[1,496,768]{2,1,0:T(8,128)}, u32[]{:S(2)}) copy-start(f32[1,496,768]{2,1,0:T(8,128)} %param.11) | copy-start | bytes 4571140
  21.9 344.5 %all-gather.7.cloned.1.call-start = ((), (), s32[]{:S(2)}) async-start(), calls=%async_computation.1 | async-start | bytes 29246976 | tf_op jit(solution)/shard_map/all_gather | solution.py:77
  21.9 21.4 %copy-start.15 = (f32[1,496,768]{2,1,0:T(8,128)S(1)}, f32[1,496,768]{2,1,0:T(8,128)}, u32[]{:S(2)}) copy-start(f32[1,496,768]{2,1,0:T(8,128)} %param.10) | copy-start | bytes 4571140
  39.2 1851.9 %all-reduce.5.cloned.1.call-start = ((), (), s32[]{:S(2)}) async-start(), calls=%async_computation.2 | async-start | bytes 113442816
  502.1 20.0 %copy-start.11 = (bf16[32,55296]{1,0:T(8,128)(2,1)S(1)}, bf16[32,55296]{1,0:T(8,128)(2,1)}, u32[]{:S(2)}) copy-start(bf16[32,55296]{1,0:T(8,128)(2,1)} %slice.370) | copy-start | bytes 10616836
  526.2 25.3 %copy-start.100 = (f32[768]{0:T(1024)}, f32[768]{0:T(1024)S(1)}, u32[]{:S(2)}) copy-start(f32[768]{0:T(1024)S(1)} %add.223) | copy-start | bytes 9220
  527.7 23.7 %copy-start.82 = (f32[768]{0:T(1024)}, f32[768]{0:T(1024)S(1)}, u32[]{:S(2)}) copy-start(f32[768]{0:T(1024)S(1)} %mul.389) | copy-start | bytes 9220
  527.7 20.6 %copy-start.28 = (f32[496,768]{1,0:T(8,128)S(1)}, f32[496,768]{1,0:T(8,128)}, u32[]{:S(2)}) copy-start(f32[496,768]{1,0:T(8,128)} %copy-done.27) | copy-start | bytes 4571140
  527.7 20.6 %copy-start.36 = (bf16[3072,32,24]{0,2,1:T(8,128)(2,1)S(1)}, bf16[3072,32,24]{0,2,1:T(8,128)(2,1)}, u32[]{:S(2)}) copy-start(bf16[3072,32,24]{0,2,1:T(8,128)(2,1)} %copy.105) | copy-start | bytes 14155780
  527.8 20.6 %copy-start.106 = (f32[768]{0:T(1024)S(1)}, f32[768]{0:T(1024)}, u32[]{:S(2)}) copy-start(f32[768]{0:T(1024)} %add.218) | copy-start | bytes 9220
  581.8 106.4 %copy-start.24 = (f32[496,768]{1,0:T(8,128)}, f32[496,768]{1,0:T(8,128)S(1)}, u32[]{:S(2)}) copy-start(f32[496,768]{1,0:T(8,128)S(1)} %get-tuple-element.116) | copy-start | bytes 4571140
  657.5 18.4 copy-start.23
  657.5 18.4 copy-start.35
  853.5 70.9 %copy-start.103 = (f32[768]{0:T(1024)S(1)}, f32[768]{0:T(1024)}, u32[]{:S(2)}) copy-start(f32[768]{0:T(1024)} %get-tuple-element.37) | copy-start | bytes 9220
  853.5 71.2 %copy-start.86 = (f32[3072]{0:T(1024)S(1)}, f32[3072]{0:T(1024)}, u32[]{:S(2)}) copy-start(f32[3072]{0:T(1024)} %get-tuple-element.126) | copy-start | bytes 36868
  853.5 71.5 %copy-start.85 = (f32[768]{0:T(1024)S(1)}, f32[768]{0:T(1024)}, u32[]{:S(2)}) copy-start(f32[768]{0:T(1024)} %get-tuple-element.57) | copy-start | bytes 9220
  853.5 71.6 %copy-start.84 = (f32[768]{0:T(1024)S(1)}, f32[768]{0:T(1024)}, u32[]{:S(2)}) copy-start(f32[768]{0:T(1024)} %get-tuple-element.75) | copy-start | bytes 9220
  853.5 71.7 %copy-start.99 = (f32[768]{0:T(1024)S(1)}, f32[768]{0:T(1024)}, u32[]{:S(2)}) copy-start(f32[768]{0:T(1024)} %get-tuple-element.45) | copy-start | bytes 9220
  975.1 71.1 %copy-start.104 = (f32[768]{0:T(1024)S(1)}, f32[768]{0:T(1024)}, u32[]{:S(2)}) copy-start(f32[768]{0:T(1024)} %get-tuple-element.33) | copy-start | bytes 9220
  975.1 71.4 %copy-start.88 = (f32[3072]{0:T(1024)S(1)}, f32[3072]{0:T(1024)}, u32[]{:S(2)}) copy-start(f32[3072]{0:T(1024)} %get-tuple-element.55) | copy-start | bytes 36868
  975.1 71.7 %copy-start.76 = (f32[768]{0:T(1024)S(1)}, f32[768]{0:T(1024)}, u32[]{:S(2)}) copy-start(f32[768]{0:T(1024)} %get-tuple-element.53) | copy-start | bytes 9220
  975.1 71.8 %copy-start.81 = (f32[768]{0:T(1024)S(1)}, f32[768]{0:T(1024)}, u32[]{:S(2)}) copy-start(f32[768]{0:T(1024)} %get-tuple-element.51) | copy-start | bytes 9220
  975.1 72.0 %copy-start.102 = (f32[768]{0:T(1024)S(1)}, f32[768]{0:T(1024)}, u32[]{:S(2)}) copy-start(f32[768]{0:T(1024)} %get-tuple-element.43) | copy-start | bytes 9220
  (117 other events, 569.4 us)
Sparse Core Ops, SparseCore 0:
  22.0 172.6 all-gather.4
  198.2 168.1 all-gather.6
  1084.7 806.3 all-reduce.4
where the time goes:
time: 1930 us; the launch traced here: 1920 us
  waiting for transfers between devices  1090 us (56%)
  local copies, waits for them, and re-layouts  599 us (31%)
  matrix products  179 us (9%)
  other arithmetic  40.2 us (2%)
    unnamed x4, waiting for transfers between devices  795 us
    all_gather x2, waiting for transfers between devices, collect(): gathered = lax.all_gather(owned_row, ('dp', 'fsdp'), axis=0, tiled=True)  291 us
    reshape x7, local copies, waits for them, and re-layouts, pack_blocks(): grad.reshape(grad.shape[0], count, -1).transpose(1, 0, 2).reshape(count, -1)  168 us
    unnamed x322, local copies, waits for them, and re-layouts  114 us
    reshape x2, local copies, waits for them, and re-layouts, unpack_whole(): section.reshape(count, shape[0], shape[1]).transpose(1, 0, 2)  111 us
    transpose x2, local copies, waits for them, and re-layouts, unpack_whole(): result.append(section.reshape(count, shape[0], shape[1]).transpose(1, 0,...  39.8 us
    dot_general x2, matrix products, forward_layer(): jnp.dot(normed_two, w_up, preferred_element_type=jnp.float32)  39 us
  transfers between devices with their start and end apart: 3, of which 3 were waited for; matrix products, arithmetic and copies ran while one was open for 3% of the time, Pallas kernels for 0%

commit v1 on v0

--- a/solution.py
+++ b/solution.py
@@ -7,6 +7,18 @@
 HEAD_WIDTH = 64
 norm_eps = 1e-06
 section_kinds = ("rows", "rows", "rows", "cols", "cols", "flat", "cols")
+
+
+def collect_2(value, axis, dim):
+    ways, here = (lax.axis_size(axis), lax.axis_index(axis))
+    grown, reach = (value, 1)
+    while reach < ways:
+        theirs = lax.ppermute(grown, axis, [(d, d ^ reach) for d in range(ways)])
+        mine_first = jnp.concatenate([grown, theirs], axis=dim)
+        theirs_first = jnp.concatenate([theirs, grown], axis=dim)
+        grown = jnp.where(here & reach == 0, mine_first, theirs_first)
+        reach = 2 * reach
+    return grown
 
 
 def layer_norm(values, gain, shift):
@@ -74,7 +86,7 @@
     pieces = (w_qkv, w_out, w_up, w_down, gains, up_shift, shifts)
     shapes = [piece.shape for piece in pieces]
     owned_row = pack_owned(pieces)
-    gathered = lax.all_gather(owned_row, ("dp", "fsdp"), axis=0, tiled=True)
+    gathered = collect_2(owned_row, ("dp", "fsdp"), 0)
     return unpack_whole(gathered, shapes)
 
 

time: 1930 us -> 2370 us (1.23)
  waiting for transfers between devices: 1090 us -> 1490 us
  other arithmetic: 40.2 us -> 101 us
  local copies, waits for them, and re-layouts: 599 us -> 569 us
    ppermute x0 -> x10, waiting for transfers between devices: none -> 691 us  [collect_2(): theirs = lax.ppermute(grown, axis, [(d, d ^ reach) for d in range(ways)])]
    all_gather x2 -> x0, waiting for transfers between devices: 291 us -> none  [collect(): gathered = lax.all_gather(owned_row, ('dp', 'fsdp'), axis=0, tiled=True)]
    select_n x0 -> x10, other arithmetic: none -> 57 us  [collect_2(): grown = jnp.where(here & reach == 0, mine_first, theirs_first)]
    unnamed x322 -> x314, local copies, waits for them, and re-layouts: 114 us -> 88.2 us
    unnamed x4 -> x2, waiting for transfers between devices: 795 us -> 796 us
  transfers between devices with their start and end apart: 3 -> 11, of which waited for: 3 -> 9; matrix products, arithmetic and copies ran while one was open for 3% -> 4% of each run, Pallas kernels for 0% -> 0%
where the time goes in v1:
time: 2370 us; the launch traced here: 2360 us
  waiting for transfers between devices  1490 us (63%)
  local copies, waits for them, and re-layouts  569 us (24%)
  matrix products  174 us (7%)
  other arithmetic  101 us (4%)
    unnamed x2, waiting for transfers between devices  796 us
    ppermute x10, waiting for transfers between devices, collect_2(): theirs = lax.ppermute(grown, axis, [(d, d ^ reach) for d in range(ways)])  691 us
    reshape x7, local copies, waits for them, and re-layouts, pack_blocks(): grad.reshape(grad.shape[0], count, -1).transpose(1, 0, 2).reshape(count, -1)  168 us
    reshape x2, local copies, waits for them, and re-layouts, unpack_whole(): section.reshape(count, shape[0], shape[1]).transpose(1, 0, 2)  111 us
    unnamed x314, local copies, waits for them, and re-layouts  88.2 us
    select_n x10, other arithmetic, collect_2(): grown = jnp.where(here & reach == 0, mine_first, theirs_first)  57 us
  transfers between devices with their start and end apart: 11, of which 9 were waited for; matrix products, arithmetic and copies ran while one was open for 4% of the time, Pallas kernels for 0%

profile of v1, /device:TPU:0, one launch (start us, length us, event | category | flops | bytes accessed | tf_op | source)
XLA Modules:
  0.0 2364.0 jit_solution(7050424908374398852)
XLA Ops:
  68.5 13.8 collective-permute-done.1
  89.4 11.2 collective-permute-done.6
  107.3 21.7 collective-permute-done.2
  135.9 28.9 %collective-permute-done.7 = bf16[4,221472]{1,0:T(4,128)(2,1)S(1)} collective-permute-done((bf16[4,221472]{1,0:T(4,128)(2,1)S(1)}, bf16[4,221472]{1,0:T(4,128)(2,1)S(1)}, u32[]{:S(2)}, u32[]{:S(2)}) %collective-permute-start.7) | collective-permute-done | bytes 1771808 | tf_op jit(solution)/shard_map/ppermute | solution.py:16
  171.1 117.2 %collective-permute-done.3 = bf16[8,221472]{1,0:T(8,128)(2,1)S(1)} collective-permute-done((bf16[8,221472]{1,0:T(8,128)(2,1)S(1)}, bf16[8,221472]{1,0:T(8,128)(2,1)S(1)}, u32[]{:S(2)}, u32[]{:S(2)}) %collective-permute-start.3) | collective-permute-done | bytes 3543584 | tf_op jit(solution)/shard_map/ppermute | solution.py:16
  294.0 66.1 %collective-permute-done.8 = bf16[8,221472]{1,0:T(8,128)(2,1)S(1)} collective-permute-done((bf16[8,221472]{1,0:T(8,128)(2,1)S(1)}, bf16[8,221472]{1,0:T(8,128)(2,1)S(1)}, u32[]{:S(2)}, u32[]{:S(2)}) %collective-permute-start.8) | collective-permute-done | bytes 3543584 | tf_op jit(solution)/shard_map/ppermute | solution.py:16
  363.5 377.6 %collective-permute-done.4 = bf16[16,221472]{1,0:T(8,128)(2,1)S(1)} collective-permute-done((bf16[16,221472]{1,0:T(8,128)(2,1)S(1)}, bf16[16,221472]{1,0:T(8,128)(2,1)S(1)}, u32[]{:S(2)}, u32[]{:S(2)}) %collective-permute-start.4) | collective-permute-done | bytes 7087136 | tf_op jit(solution)/shard_map/ppermute | solution.py:16
  741.1 9.3 maximum_select_fusion
  762.5 54.8 %collective-permute-done.9 = bf16[16,221472]{1,0:T(8,128)(2,1)} collective-permute-done((bf16[16,221472]{1,0:T(8,128)(2,1)S(1)}, bf16[16,221472]{1,0:T(8,128)(2,1)}, u32[]{:S(2)}, u32[]{:S(2)}) %collective-permute-start.9) | collective-permute-done | bytes 7087136 | tf_op jit(solution)/shard_map/ppermute | solution.py:16
  817.2 9.8 maximum_select_fusion.1
  832.1 8.2 fusion.77
  890.1 55.3 %reshape.869 = bf16[32,3072,24]{2,1,0:T(8,128)(2,1)} reshape(bf16[32,73728]{1,0:T(8,128)(2,1)} %get-tuple-element.73) | data formatting | bytes 9437184 | tf_op jit(solution)/shard_map/reshape | solution.py:52
  945.4 20.0 copy.105
  971.2 20.5 multiply_convert_fusion.3
  1024.4 55.5 %reshape.878 = bf16[32,3072,24]{2,1,0:T(8,128)(2,1)} reshape(bf16[32,73728]{1,0:T(8,128)(2,1)} %get-tuple-element.71) | data formatting | bytes 9437184 | tf_op jit(solution)/shard_map/reshape | solution.py:52
  1079.9 19.8 copy.119
  1099.7 18.5 multiply_convert_fusion.2
  1268.6 25.8 %copy.136 = f32[32,3072,24]{2,1,0:T(8,128)} copy(f32[32,3072,24]{1,0,2:T(8,128)} %convolution_bitcast_fusion) | data formatting | bytes 18874368 | tf_op jit(solution)/shard_map/transpose | solution.py:66
  1294.4 70.9 %reshape.896 = f32[32,73728]{1,0:T(8,128)} reshape(f32[32,3072,24]{2,1,0:T(8,128)} %copy.136) | data formatting | bytes 18874368 | tf_op jit(solution)/shard_map/reshape | solution.py:66
  1390.3 25.7 %copy.129 = f32[3072,32,24]{2,0,1:T(8,128)} copy(f32[3072,32,24]{0,2,1:T(8,128)} %bitcast.262) | data formatting | bytes 18874368 | tf_op jit(solution)/shard_map/reshape | solution.py:66
  1416.0 71.3 %reshape.889 = f32[32,73728]{1,0:T(8,128)} reshape(f32[32,3072,24]{2,1,0:T(8,128)} %bitcast.241) | data formatting | bytes 18874368 | tf_op jit(solution)/shard_map/reshape | solution.py:66
  1490.1 8.5 constant_dynamic-update-slice_fusion.25
  1508.8 8.5 constant_dynamic-update-slice_fusion.15
  1537.5 795.7 %all-reduce.5.cloned.1.call-done = (f32[32,221472]{1,0:T(8,128)}, f32[32,221472]{1,0:T(8,128)}) async-done(((f32[32,221472]{1,0:T(8,128)}, f32[32,221472]{1,0:T(8,128)}), (f32[32,221472]{1,0:T(8,128)}, f32[32,221472]{1,0:T(8,128)})) %all-reduce.5.cloned.1.call-update) | async-done | bytes 56696848
  (575 shorter events, 432.7 us)
Async XLA Ops:
  7.2 2326.0 %all-reduce.5.cloned.1.call-start = ((), (), s32[]{:S(2)}) async-start(), calls=%async_computation | async-start | bytes 113442816
  13.0 32.9 %copy-start.14 = (f32[1,496,768]{2,1,0:T(8,128)S(1)}, f32[1,496,768]{2,1,0:T(8,128)}, u32[]{:S(2)}) copy-start(f32[1,496,768]{2,1,0:T(8,128)} %param.10) | copy-start | bytes 4571140
  28.9 22.5 collective-permute-start
  45.8 16.0 collective-permute-start.5
  50.9 54.6 %copy-start.70 = (f32[496]{0:T(512)}, f32[496]{0:T(512)S(1)}, u32[]{:S(2)}) copy-start(f32[496]{0:T(512)S(1)} %multiply_reduce_fusion.13) | copy-start | bytes 5956
  58.8 23.5 collective-permute-start.1
  68.4 32.2 %collective-permute-start.6 = (bf16[2,221472]{1,0:T(2,128)(2,1)S(1)}, bf16[2,221472]{1,0:T(2,128)(2,1)S(1)}, u32[]{:S(2)}, u32[]{:S(2)}) collective-permute-start(bf16[2,221472]{1,0:T(2,128)(2,1)S(1)} %broadcast_select_fusion), channel_id=1, source_target_pairs={{0,2},{1,3},{2,0},{3,1},{4,6},{5,7},{6,4},{7,5},{8,10},{9,11},{10,... | collective-permute-start | bytes 2657672 | tf_op jit(solution)/shard_map/ppermute | solution.py:16
  87.3 41.7 %collective-permute-start.2 = (bf16[4,221472]{1,0:T(4,128)(2,1)S(1)}, bf16[4,221472]{1,0:T(4,128)(2,1)S(1)}, u32[]{:S(2)}, u32[]{:S(2)}) collective-permute-start(bf16[4,221472]{1,0:T(4,128)(2,1)S(1)} %maximum_select_fusion.6), channel_id=1, source_target_pairs={{0,4},{1,5},{2,6},{3,7},{4,0},{5,1},{6,2},{7,3},{8,12},{9,13},{10,... | collective-permute-start | bytes 5315336 | tf_op jit(solution)/shard_map/ppermute | solution.py:16
  105.5 59.3 %collective-permute-start.7 = (bf16[4,221472]{1,0:T(4,128)(2,1)S(1)}, bf16[4,221472]{1,0:T(4,128)(2,1)S(1)}, u32[]{:S(2)}, u32[]{:S(2)}) collective-permute-start(bf16[4,221472]{1,0:T(4,128)(2,1)S(1)} %maximum_select_fusion.7), channel_id=1, source_target_pairs={{0,4},{1,5},{2,6},{3,7},{4,0},{5,1},{6,2},{7,3},{8,12},{9,13},{10,... | collective-permute-start | bytes 5315336 | tf_op jit(solution)/shard_map/ppermute | solution.py:16
  133.7 154.5 %collective-permute-start.3 = (bf16[8,221472]{1,0:T(8,128)(2,1)S(1)}, bf16[8,221472]{1,0:T(8,128)(2,1)S(1)}, u32[]{:S(2)}, u32[]{:S(2)}) collective-permute-start(bf16[8,221472]{1,0:T(8,128)(2,1)S(1)} %maximum_select_fusion.4), channel_id=1, source_target_pairs={{0,8},{1,9},{2,10},{3,11},{4,12},{5,13},{6,14},{7,15},{8,0},{9,1},... | collective-permute-start | bytes 10630664 | tf_op jit(solution)/shard_map/ppermute | solution.py:16
  169.5 190.6 %collective-permute-start.8 = (bf16[8,221472]{1,0:T(8,128)(2,1)S(1)}, bf16[8,221472]{1,0:T(8,128)(2,1)S(1)}, u32[]{:S(2)}, u32[]{:S(2)}) collective-permute-start(bf16[8,221472]{1,0:T(8,128)(2,1)S(1)} %maximum_select_fusion.5), channel_id=1, source_target_pairs={{0,8},{1,9},{2,10},{3,11},{4,12},{5,13},{6,14},{7,15},{8,0},{9,1},... | collective-permute-start | bytes 10630664 | tf_op jit(solution)/shard_map/ppermute | solution.py:16
  290.6 450.5 %collective-permute-start.4 = (bf16[16,221472]{1,0:T(8,128)(2,1)S(1)}, bf16[16,221472]{1,0:T(8,128)(2,1)S(1)}, u32[]{:S(2)}, u32[]{:S(2)}) collective-permute-start(bf16[16,221472]{1,0:T(8,128)(2,1)S(1)} %maximum_select_fusion.2), channel_id=1, source_target_pairs={{0,16},{1,17},{2,18},{3,19},{4,20},{5,21},{6,22},{7,23},{8,24},{9,... | collective-permute-start | bytes 21261320 | tf_op jit(solution)/shard_map/ppermute | solution.py:16
  362.5 454.8 %collective-permute-start.9 = (bf16[16,221472]{1,0:T(8,128)(2,1)S(1)}, bf16[16,221472]{1,0:T(8,128)(2,1)}, u32[]{:S(2)}, u32[]{:S(2)}) collective-permute-start(bf16[16,221472]{1,0:T(8,128)(2,1)S(1)} %maximum_select_fusion.3), channel_id=1, source_target_pairs={{0,16},{1,17},{2,18},{3,19},{4,20},{5,21},{6,22},{7,23},{8,24},{9,... | collective-permute-start | bytes 21261320 | tf_op jit(solution)/shard_map/ppermute | solution.py:16
  1024.1 106.3 %copy-start.23 = (f32[496,768]{1,0:T(8,128)}, f32[496,768]{1,0:T(8,128)S(1)}, u32[]{:S(2)}) copy-start(f32[496,768]{1,0:T(8,128)S(1)} %get-tuple-element.116) | copy-start | bytes 4571140
  1294.4 70.9 %copy-start.101 = (f32[768]{0:T(1024)S(1)}, f32[768]{0:T(1024)}, u32[]{:S(2)}) copy-start(f32[768]{0:T(1024)} %get-tuple-element.37) | copy-start | bytes 9220
  1294.4 71.2 %copy-start.86 = (f32[3072]{0:T(1024)S(1)}, f32[3072]{0:T(1024)}, u32[]{:S(2)}) copy-start(f32[3072]{0:T(1024)} %get-tuple-element.126) | copy-start | bytes 36868
  1294.4 71.5 %copy-start.85 = (f32[768]{0:T(1024)S(1)}, f32[768]{0:T(1024)}, u32[]{:S(2)}) copy-start(f32[768]{0:T(1024)} %get-tuple-element.57) | copy-start | bytes 9220
  1294.4 71.6 %copy-start.84 = (f32[768]{0:T(1024)S(1)}, f32[768]{0:T(1024)}, u32[]{:S(2)}) copy-start(f32[768]{0:T(1024)} %get-tuple-element.75) | copy-start | bytes 9220
  1294.4 71.8 %copy-start.97 = (f32[768]{0:T(1024)S(1)}, f32[768]{0:T(1024)}, u32[]{:S(2)}) copy-start(f32[768]{0:T(1024)} %get-tuple-element.45) | copy-start | bytes 9220
  1416.0 71.3 %copy-start.102 = (f32[768]{0:T(1024)S(1)}, f32[768]{0:T(1024)}, u32[]{:S(2)}) copy-start(f32[768]{0:T(1024)} %get-tuple-element.33) | copy-start | bytes 9220
  1416.0 71.7 %copy-start.57 = (f32[3072]{0:T(1024)S(1)}, f32[3072]{0:T(1024)}, u32[]{:S(2)}) copy-start(f32[3072]{0:T(1024)} %get-tuple-element.55) | copy-start | bytes 36868
  1416.0 71.9 %copy-start.76 = (f32[768]{0:T(1024)S(1)}, f32[768]{0:T(1024)}, u32[]{:S(2)}) copy-start(f32[768]{0:T(1024)} %get-tuple-element.53) | copy-start | bytes 9220
  1416.0 72.0 %copy-start.81 = (f32[768]{0:T(1024)S(1)}, f32[768]{0:T(1024)}, u32[]{:S(2)}) copy-start(f32[768]{0:T(1024)} %get-tuple-element.51) | copy-start | bytes 9220
  1416.0 72.2 %copy-start.100 = (f32[768]{0:T(1024)S(1)}, f32[768]{0:T(1024)}, u32[]{:S(2)}) copy-start(f32[768]{0:T(1024)} %get-tuple-element.43) | copy-start | bytes 9220
  (126 other events, 808.2 us)
Sparse Core Ops, SparseCore 0:
  1526.0 807.2 all-reduce.4
